TPU v7x, 128 devices: a whole 4x4x4 slice. The times are simulated.
128 devices in a mesh: dp: 16 (over z, x_lo, core), ctx: 8 (over x_hi, y).
Axes of the slice: x: 4 (x_hi: 2, x_lo: 2; x = x_hi * 2 + x_lo), y: 4, z: 4, core: 2. Of those that a mesh axis runs over, the one named last changes fastest.
Arguments:
- hidden: bfloat16 [16, 1024, 4096], P('dp', 'ctx'), may hold values from -6 to 6
- queries: bfloat16 [16, 1024, 4096], P('dp', 'ctx'), may hold values from -6 to 6
- keys: bfloat16 [16, 1024, 256], P('dp', 'ctx'), may hold values from -6 to 6
- values: bfloat16 [16, 1024, 256], P('dp', 'ctx'), may hold values from -24 to 24
- out_weight: bfloat16 [4096, 4096], P(None, 'ctx'), may hold values from -0.09375 to 0.09375
- norm_gain: float32 [4096], replicated, may hold values from 0.1 to 1.9
- routes: int32 [16, 1024, 8], P('dp', 'ctx'), may hold values from 0 to 127, all different within a row; in each aligned block of 128 rows (0 to 127, 128 to 255, ..., all dimensions but the last counted through in order) at most 9 rows name the same one
- slot_scores: float32 [16, 1024, 8], P('dp', 'ctx'), may hold values from 0.1 to 1
- gate_weight: bfloat16 [128, 4096, 768], P(('dp', 'ctx')), may hold values from -0.09375 to 0.09375
- up_weight: bfloat16 [128, 4096, 768], P(('dp', 'ctx')), may hold values from -0.09375 to 0.09375
- down_weight: bfloat16 [128, 768, 4096], P(('dp', 'ctx')), may hold values from -0.21875 to 0.21875
Outputs:
- output: bfloat16 [16, 1024, 4096], P('dp', 'ctx')
Inputs may be any that keep to these rules, and one draw needn't show every extreme that they name: In each aligned block of 128 tokens (the tokens of one device, sequences in order) no expert is named by more than 9 of the block's routes, a bound that some block reaches.
All inputs are finite; a program needn't handle non-finite values.
Results may differ from a plain program's by a relative error of at most 0.0065.
Values may be sent and summed in bfloat16 or wider, within the bound.
No kernel may reach another device: no remote copies, remote signals or barrier semaphores. Data moves between devices by JAX's collectives and lax.ppermute only.
A program may use at most 192 MiB of HBM per device.

v0:
```python
import jax
import jax.numpy as jnp
from jax import lax
from jax.sharding import PartitionSpec as P

HQ = 32
KVH = 2
DH = 128
TOP = 8


def expert_ffn(slots_in, w_gate, w_up, w_down):
    flat_rows = slots_in.reshape(-1, slots_in.shape[-1])
    gated = jnp.dot(flat_rows, w_gate, preferred_element_type=jnp.float32)
    lifted = jnp.dot(flat_rows, w_up, preferred_element_type=jnp.float32)
    activated = (jax.nn.silu(gated) * lifted).astype(jnp.bfloat16)
    result = jnp.dot(activated, w_down, preferred_element_type=jnp.float32).astype(jnp.bfloat16)
    return result.reshape(slots_in.shape)


def local(
    hidden,
    queries,
    keys,
    values,
    out_weight,
    norm_gain,
    routes,
    slot_scores,
    gate_weight,
    up_weight,
    down_weight,
):
    tok_count = hidden.shape[1]
    model_width = hidden.shape[2]
    group_size = HQ // KVH
    score_scale = DH ** (-0.5)
    ctx_index = lax.axis_index("ctx")
    query_rows = queries[0].reshape(tok_count, KVH, group_size, DH)
    query_pos = ctx_index * tok_count + jnp.arange(tok_count, dtype=jnp.int32)
    key_piece = lax.all_gather(keys, "ctx", axis=1, tiled=True)
    value_piece = lax.all_gather(values, "ctx", axis=1, tiled=True)
    key_count = key_piece.shape[1]
    key_rows = key_piece[0].reshape(key_count, KVH, DH)
    value_rows = value_piece[0].reshape(key_count, KVH, DH)
    key_pos = jnp.arange(key_count, dtype=jnp.int32)
    running_max = jnp.full((KVH, group_size, tok_count), -1e30, jnp.float32)
    scores = (
        jnp.einsum("qkgd,jkd->kgqj", query_rows, key_rows, preferred_element_type=jnp.float32)
        * score_scale
    )
    causal = key_pos[None, :] <= query_pos[:, None]
    scores = jnp.where(causal, scores, -1e30)
    new_max = jnp.maximum(running_max, jnp.max(scores, axis=-1))
    weights = jnp.where(causal, jnp.exp(scores - new_max[..., None]), 0.0)
    running_sum = jnp.sum(weights, axis=-1)
    numerator = jnp.einsum(
        "kgqj,jkd->kgqd",
        weights.astype(jnp.bfloat16),
        value_rows,
        preferred_element_type=jnp.float32,
    )
    running_max, running_sum, numerator = (new_max, running_sum, numerator)
    attended = numerator / running_sum[..., None]
    attended = (
        jnp.transpose(attended, (2, 0, 1, 3)).reshape(tok_count, HQ * DH).astype(jnp.bfloat16)
    )
    columns = jnp.dot(
        lax.all_gather(attended, "ctx", axis=0, tiled=True),
        out_weight,
        preferred_element_type=jnp.float32,
    ).astype(jnp.bfloat16)
    projected = lax.all_to_all(columns, "ctx", split_axis=0, concat_axis=1, tiled=True)
    residual = hidden[0].astype(jnp.float32) + projected.astype(jnp.float32)
    normed = (
        residual
        * lax.rsqrt(jnp.mean(residual * residual, axis=1, keepdims=True) + 1e-06)
        * norm_gain
    ).astype(jnp.bfloat16)
    score_rows = slot_scores[0]
    slot_gates = score_rows / jnp.sum(score_rows, axis=1, keepdims=True)
    expert_total = lax.axis_size(("dp", "ctx"))
    capacity = max(2, tok_count * TOP * 9 // (8 * expert_total))
    expert_ids = routes[0].reshape(tok_count * TOP)
    one_hot = (expert_ids[:, None] == jnp.arange(expert_total, dtype=jnp.int32)[None, :]).astype(
        jnp.int32
    )
    earlier = jnp.sum((jnp.cumsum(one_hot, axis=0) - one_hot) * one_hot, axis=1)
    slot_index = expert_ids * capacity + earlier
    token_of = jnp.arange(tok_count * TOP, dtype=jnp.int32) // TOP
    outgoing = (
        jnp.zeros((expert_total * capacity, model_width), jnp.bfloat16)
        .at[slot_index]
        .set(normed[token_of])
    )
    outgoing = outgoing.reshape(expert_total, capacity, model_width)
    served = expert_ffn(
        lax.all_to_all(outgoing, ("dp", "ctx"), split_axis=0, concat_axis=0, tiled=True),
        gate_weight[0],
        up_weight[0],
        down_weight[0],
    )
    returned = lax.all_to_all(served, ("dp", "ctx"), split_axis=0, concat_axis=0, tiled=True)
    returned = returned.reshape(expert_total * capacity, model_width)
    picked = returned[slot_index].reshape(tok_count, TOP, model_width)
    mixture = jnp.sum(slot_gates[:, :, None] * picked.astype(jnp.float32), axis=1)
    return (residual + mixture).astype(jnp.bfloat16)[None]


def solution(mesh):
    return jax.shard_map(
        local,
        mesh=mesh,
        in_specs=(
            P("dp", "ctx", None),
            P("dp", "ctx", None),
            P("dp", "ctx", None),
            P("dp", "ctx", None),
            P(None, "ctx"),
            P(),
            P("dp", "ctx", None),
            P("dp", "ctx", None),
            P(("dp", "ctx"), None, None),
            P(("dp", "ctx"), None, None),
            P(("dp", "ctx"), None, None),
        ),
        out_specs=P("dp", "ctx", None),
        check_vma=False,
    )
```

profile of v0, /device:TPU:91, one launch (start us, length us, event | category | flops | bytes accessed | tf_op | source)
XLA Modules:
  0.0 829.0 jit_solution(7543872358024971029)
XLA Ops:
  6.5 29.6 %all_gather.10 = bf16[1,1024,256]{2,1,0:T(8,128)(2,1)S(1)} all-gather(bf16[1,128,256]{2,1,0:T(8,128)(2,1)} %param.14), channel_id=1, replica_groups=mesh['dp'=16,'ctx'=8] {'ctx'}, dimensions={1}, use_global_device_ids=true | all-gather | bytes 589824 | tf_op jit(solution)/shard_map/all_gather | solution.py:42
  36.5 1.0 copy.18
  37.5 25.4 %all_gather.9 = bf16[1,1024,256]{1,2,0:T(8,128)(2,1)S(1)} all-gather(bf16[1,128,256]{1,2,0:T(8,128)(2,1)S(1)} %copy.18), channel_id=1, replica_groups=mesh['dp'=16,'ctx'=8] {'ctx'}, dimensions={1}, use_global_device_ids=true | all-gather | bytes 589824 | tf_op jit(solution)/shard_map/all_gather | solution.py:41
  62.9 1.5 copy.37
  64.3 2.9 fusion.1
  67.3 4.1 fusion.2
  71.4 5.1 fusion.23
  77.4 118.9 %all-gather.2.cloned.1.call-done = bf16[1024,4096]{0,1:T(8,128)(2,1)} async-done(((bf16[128,4096]{0,1:T(8,128)(2,1)}), bf16[1024,4096]{0,1:T(8,128)(2,1)}) %all-gather.2.cloned.1.call-update) | async-done | bytes 8388624 | tf_op jit(solution)/shard_map/all_gather | solution.py:69
  196.4 10.1 %convolution_convert_fusion.1 = bf16[1024,512]{1,0:T(8,128)(2,1)} fusion(bf16[1024,4096]{0,1:T(8,128)(2,1)} %all-gather.2.cloned.1.call-done, bf16[4096,512]{1,0:T(8,128)(2,1)} %param.15), kind=kOutput, calls=%fused_computation.33 | convolution fusion | flops 4295491584 | bytes 13631488 | tf_op jit(solution)/shard_map/dot_general | solution.py:68
  206.4 6.2 all-to-all-start
  212.8 0.4 fusion.29
  213.2 12.8 %all-to-all-done = bf16[8,128,512]{2,1,0:T(8,128)(2,1)S(1)} async-done(((bf16[8,128,512]{2,1,0:T(8,128)(2,1)}), bf16[8,128,512]{2,1,0:T(8,128)(2,1)S(1)}, u32[]{:S(2)}, u32[]{:S(2)}) %all-to-all-start) | async-done | bytes 1048608 | tf_op jit(solution)/shard_map/all_to_all | solution.py:73
  226.0 1.6 convert_bitcast_fusion
  227.9 0.4 multiply_reduce_fusion
  228.3 0.4 multiply_convert_fusion
  228.7 7.7 gather_fusion
  236.5 18.4 %scatter_custom_fusion = bf16[1152,4096]{1,0:T(8,128)(2,1)} fusion(s32[1024]{0:T(1024)S(1)} %bitcast.96, bf16[1024,4096]{1,0:T(8,128)(2,1)} %gather_fusion, bf16[]{:T(256)} %constant.43.clone.1), kind=kCustom, calls=%fused_computation.18 | custom fusion | bytes 9437696 | tf_op jit(solution)/shard_map/scatter | solution.py:94
  254.9 15.1 %reshape.163 = bf16[128,9,4096]{2,1,0:T(8,128)(2,1)} reshape(bf16[1152,4096]{1,0:T(8,128)(2,1)} %scatter_custom_fusion) | data formatting | bytes 18874368 | tf_op jit(solution)/shard_map/reshape | solution.py:96
  270.0 197.8 %all_to_all.23 = bf16[128,9,4096]{2,1,0:T(8,128)(2,1)} all-to-all(bf16[128,9,4096]{2,1,0:T(8,128)(2,1)} %reshape.163), channel_id=1, replica_groups=mesh['dp'=16,'ctx'=8] {'dp','ctx'}, dimensions={0} | all-to-all | bytes 18874368 | tf_op jit(solution)/shard_map/all_to_all | solution.py:98
  467.7 15.8 %reshape.164 = bf16[1152,4096]{1,0:T(8,128)(2,1)} reshape(bf16[128,9,4096]{2,1,0:T(8,128)(2,1)} %all_to_all.23) | data formatting | bytes 18874368 | tf_op jit(solution)/shard_map/reshape | solution.py:13
  483.6 12.0 %fusion.10 = f32[1152,768]{1,0:T(8,128)S(1)} fusion(bf16[1152,4096]{1,0:T(8,128)(2,1)} %reshape.164, bf16[1,4096,768]{2,1,0:T(8,128)(2,1)} %param.19), kind=kOutput, calls=%fused_computation.16 | convolution fusion | flops 7247757312 | bytes 19267584 | tf_op jit(solution)/shard_map/dot_general | solution.py:14
  495.6 10.3 %fusion.17 = bf16[1152,768]{1,0:T(8,128)(2,1)S(1)} fusion(bf16[1152,4096]{1,0:T(8,128)(2,1)S(1)} %copy-done, bf16[1,4096,768]{2,1,0:T(8,128)(2,1)} %param.20, f32[1152,768]{1,0:T(8,128)S(1)} %fusion.10), kind=kOutput, calls=%fused_computation.21 | convolution fusion | flops 7253065728 | bytes 21037056 | tf_op jit(solution)/shard_map/dot_general | solution.py:15
  505.9 9.6 %convolution_convert_fusion = bf16[1152,4096]{1,0:T(8,128)(2,1)} fusion(bf16[1152,768]{1,0:T(8,128)(2,1)S(1)} %fusion.17, bf16[1,768,4096]{2,1,0:T(8,128)(2,1)S(1)} %bitcast.101), kind=kOutput, calls=%fused_computation.7 | convolution fusion | flops 7252475904 | bytes 17498112 | tf_op jit(solution)/shard_map/dot_general | solution.py:17
  515.5 15.1 %reshape.165 = bf16[128,9,4096]{2,1,0:T(8,128)(2,1)} reshape(bf16[1152,4096]{1,0:T(8,128)(2,1)} %convolution_convert_fusion) | data formatting | bytes 18874368 | tf_op jit(solution)/shard_map/reshape | solution.py:18
  530.6 9.5 %all-to-all-start.2 = ((bf16[128,9,4096]{2,1,0:T(8,128)(2,1)}), bf16[128,9,4096]{2,1,0:T(8,128)(2,1)}, u32[]{:S(2)}, u32[]{:S(2)}) async-start(bf16[128,9,4096]{2,1,0:T(8,128)(2,1)} %reshape.165), calls=%async_computation.2 | async-start | bytes 33554432 | tf_op jit(solution)/shard_map/all_to_all | solution.py:103
  540.3 4.2 copy.23
  544.5 2.7 reshape.167
  547.2 222.0 %all-to-all-done.2 = bf16[128,9,4096]{2,1,0:T(8,128)(2,1)} async-done(((bf16[128,9,4096]{2,1,0:T(8,128)(2,1)}), bf16[128,9,4096]{2,1,0:T(8,128)(2,1)}, u32[]{:S(2)}, u32[]{:S(2)}) %all-to-all-start.2) | async-done | bytes 9437216 | tf_op jit(solution)/shard_map/all_to_all | solution.py:103
  769.3 15.8 %reshape.166 = bf16[1152,4096]{1,0:T(8,128)(2,1)} reshape(bf16[128,9,4096]{2,1,0:T(8,128)(2,1)} %all-to-all-done.2) | data formatting | bytes 18874368 | tf_op jit(solution)/shard_map/reshape | solution.py:104
  785.1 20.0 %gather_fusion.1 = bf16[1024,4096]{1,0:T(8,128)(2,1)} fusion(bf16[1152,4096]{1,0:T(8,128)(2,1)} %reshape.166, s32[1024]{0:T(1024)S(1)} %broadcast_clamp_fusion), kind=kCustom, calls=%fused_computation.1 | custom fusion | bytes 16781312 | tf_op jit(solution)/shard_map/gather | solution.py:105
  805.0 13.2 %fusion = f32[128,4096]{1,0:T(8,128)} fusion(bf16[1024,4096]{1,0:T(8,128)(2,1)} %gather_fusion.1, f32[128,8]{1,0:T(8,128)S(1)} %copy.24), kind=kLoop, calls=%fused_computation.4 | loop fusion | flops 12058624 | bytes 10489856 | tf_op jit(solution)/shard_map/reduce_sum | solution.py:106
  818.2 3.5 fusion.21
  (43 shorter events, 1.7 us)
Async XLA Ops:
  6.5 189.8 %all-gather.2.cloned.1.call-start = ((), (), s32[]{:S(2)}) async-start(), calls=%async_computation.3 | async-start | bytes 9437184 | tf_op jit(solution)/shard_map/all_gather | solution.py:69
  71.4 5.2 copy-start.3
  206.4 21.5 %copy-start.1 = (bf16[1,128,4096]{2,1,0:T(8,128)(2,1)S(1)}, bf16[1,128,4096]{2,1,0:T(8,128)(2,1)}, u32[]{:S(2)}) copy-start(bf16[1,128,4096]{2,1,0:T(8,128)(2,1)} %param.11) | copy-start | bytes 3145732
  206.4 21.9 %copy-start.2 = (f32[4096]{0:T(1024)S(1)}, f32[4096]{0:T(1024)}, u32[]{:S(2)}) copy-start(f32[4096]{0:T(1024)} %param.16) | copy-start | bytes 49156
  206.4 19.6 %all-to-all-start = ((bf16[8,128,512]{2,1,0:T(8,128)(2,1)}), bf16[8,128,512]{2,1,0:T(8,128)(2,1)S(1)}, u32[]{:S(2)}, u32[]{:S(2)}) async-start(bf16[8,128,512]{2,1,0:T(8,128)(2,1)} %bitcast.93), calls=%async_computation | async-start | bytes 2097152 | tf_op jit(solution)/shard_map/all_to_all | solution.py:73
  483.6 12.0 %copy-start = (bf16[1152,4096]{1,0:T(8,128)(2,1)S(1)}, bf16[1152,4096]{1,0:T(8,128)(2,1)}, u32[]{:S(2)}) copy-start(bf16[1152,4096]{1,0:T(8,128)(2,1)} %reshape.164) | copy-start | bytes 28311556
  483.6 22.3 %slice-start = ((s8[6291456]{0:T(1024)(128)(4,1)}), s8[4194304]{0:T(1024)(128)(4,1)S(1)}, s32[]{:S(2)}) async-start(s8[6291456]{0:T(1024)(128)(4,1)} %bitcast.100), calls=%async_computation.4 | async-start | bytes 8388608
  495.6 10.3 %slice-start.1 = ((s8[6291456]{0:T(1024)(128)(4,1)}), s8[2097152]{0:T(1024)(128)(4,1)S(1)}, s32[]{:S(2)}) async-start(s8[6291456]{0:T(1024)(128)(4,1)} %bitcast.100), calls=%async_computation.5 | async-start | bytes 4194304
  530.6 9.6 %copy-start.4 = (f32[1,128,8]{1,2,0:T(8,128)S(1)}, f32[1,128,8]{1,2,0:T(8,128)}, u32[]{:S(2)}) copy-start(f32[1,128,8]{1,2,0:T(8,128)} %param.18) | copy-start | bytes 12292
  530.6 238.7 %all-to-all-start.2 = ((bf16[128,9,4096]{2,1,0:T(8,128)(2,1)}), bf16[128,9,4096]{2,1,0:T(8,128)(2,1)}, u32[]{:S(2)}, u32[]{:S(2)}) async-start(bf16[128,9,4096]{2,1,0:T(8,128)(2,1)} %reshape.165), calls=%async_computation.2 | async-start | bytes 33554432 | tf_op jit(solution)/shard_map/all_to_all | solution.py:103
Sparse Core Ops, SparseCore 0:
  76.7 119.6 all-gather.1
where the time goes:
time: 839 us; the launch traced here: 829 us
  waiting for transfers between devices  354 us (42%)
  blocking collectives  253 us (30%)
  local copies, waits for them, and re-layouts  119 us (14%)
  matrix products  49.9 us (6%)
  other arithmetic  24.1 us (3%)
  starting transfers between devices  15.8 us (2%)
  between operations  14.1 us (2%)
    all_to_all x1, waiting for transfers between devices, local(): lax.all_to_all(served, ('dp', 'ctx'), split_axis=0, concat_axis=0, tiled=...  222 us
    all_to_all x1, blocking collectives, local(): lax.all_to_all(outgoing, ('dp', 'ctx'), split_axis=0, concat_axis=0, tile...  198 us
    all_gather x1, waiting for transfers between devices, local(): lax.all_gather(attended, 'ctx', axis=0, tiled=True)  119 us
    all_gather x1, blocking collectives, local(): value_piece = lax.all_gather(values, 'ctx', axis=1, tiled=True)  29.6 us
    all_gather x1, blocking collectives, local(): key_piece = lax.all_gather(keys, 'ctx', axis=1, tiled=True)  25.4 us
    gather x1, local copies, waits for them, and re-layouts, local(): picked = returned[slot_index].reshape(tok_count, TOP, model_width)  20 us
    scatter x1, local copies, waits for them, and re-layouts, local(): outgoing = jnp.zeros((expert_total * capacity, model_width), jnp.bfloat16...  18.4 us
  transfers between devices with their start and end apart: 3, of which 3 were waited for; matrix products, arithmetic and copies ran while one was open for 1% of the time, Pallas kernels for 0%

commit v1 on v0

--- a/solution.py
+++ b/solution.py
@@ -66,7 +66,9 @@
         jnp.transpose(attended, (2, 0, 1, 3)).reshape(tok_count, HQ * DH).astype(jnp.bfloat16)
     )
     columns = jnp.dot(
-        lax.all_gather(attended, "ctx", axis=0, tiled=True),
+        jnp.concatenate(
+            lax.all_to_all(jnp.stack([attended] * lax.axis_size("ctx")), "ctx", 0, 0), axis=0
+        ),
         out_weight,
         preferred_element_type=jnp.float32,
     ).astype(jnp.bfloat16)

time: 839 us -> 809 us (0.964)
  waiting for transfers between devices: 354 us -> 325 us
  between operations: 14.1 us -> 0.68 us
  starting transfers between devices: 15.8 us -> 24.7 us
    all_gather x1 -> x0, waiting for transfers between devices: 119 us -> none  [local(): lax.all_gather(attended, 'ctx', axis=0, tiled=True)]
    all_to_all x0 -> x1, waiting for transfers between devices: none -> 89.5 us  [local(): lax.all_to_all(jnp.stack([attended] * lax.axis_size('ctx')), 'ctx', 0, 0)]
where the time goes in v1:
time: 809 us; the launch traced here: 799 us
  waiting for transfers between devices  325 us (40%)
  blocking collectives  252 us (31%)
  local copies, waits for them, and re-layouts  123 us (15%)
  matrix products  49.1 us (6%)
  starting transfers between devices  24.7 us (3%)
  other arithmetic  24.1 us (3%)
    all_to_all x1, waiting for transfers between devices, local(): lax.all_to_all(served, ('dp', 'ctx'), split_axis=0, concat_axis=0, tiled=...  222 us
    all_to_all x1, blocking collectives, local(): lax.all_to_all(outgoing, ('dp', 'ctx'), split_axis=0, concat_axis=0, tile...  197 us
    all_to_all x1, waiting for transfers between devices, local(): lax.all_to_all(jnp.stack([attended] * lax.axis_size('ctx')), 'ctx', 0, 0)  89.5 us
    all_gather x1, blocking collectives, local(): value_piece = lax.all_gather(values, 'ctx', axis=1, tiled=True)  29.6 us
    all_gather x1, blocking collectives, local(): key_piece = lax.all_gather(keys, 'ctx', axis=1, tiled=True)  25.4 us
    gather x1, local copies, waits for them, and re-layouts, local(): picked = returned[slot_index].reshape(tok_count, TOP, model_width)  20 us
    scatter x1, local copies, waits for them, and re-layouts, local(): outgoing = jnp.zeros((expert_total * capacity, model_width), jnp.bfloat16...  18.4 us
  transfers between devices with their start and end apart: 3, of which 3 were waited for; matrix products, arithmetic and copies ran while one was open for 1% of the time, Pallas kernels for 0%

profile of v1, /device:TPU:91, one launch (start us, length us, event | category | flops | bytes accessed | tf_op | source)
XLA Modules:
  0.0 799.4 jit_solution(5962564455281677067)
XLA Ops:
  0.0 29.6 %all_gather.7 = bf16[1,1024,256]{2,1,0:T(8,128)(2,1)S(1)} all-gather(bf16[1,128,256]{2,1,0:T(8,128)(2,1)} %param.14), channel_id=1, replica_groups=mesh['dp'=16,'ctx'=8] {'ctx'}, dimensions={1}, use_global_device_ids=true | all-gather | bytes 589824 | tf_op jit(solution)/shard_map/all_gather | solution.py:42
  30.0 1.0 copy.19
  30.9 25.4 %all_gather.6 = bf16[1,1024,256]{1,2,0:T(8,128)(2,1)S(1)} all-gather(bf16[1,128,256]{1,2,0:T(8,128)(2,1)S(1)} %copy.19), channel_id=1, replica_groups=mesh['dp'=16,'ctx'=8] {'ctx'}, dimensions={1}, use_global_device_ids=true | all-gather | bytes 589824 | tf_op jit(solution)/shard_map/all_gather | solution.py:41
  56.3 1.5 copy.39
  57.8 2.9 fusion.1
  60.7 4.1 fusion.2
  64.9 4.4 fusion.23
  69.2 0.5 copy.24
  69.8 4.3 stack.2
  74.1 6.0 all-to-all-start
  81.0 89.5 %all-to-all-done = bf16[8,128,4096]{2,1,0:T(8,128)(2,1)} async-done(((bf16[8,128,4096]{2,1,0:T(8,128)(2,1)}), bf16[8,128,4096]{2,1,0:T(8,128)(2,1)}, u32[]{:S(2)}, u32[]{:S(2)}) %all-to-all-start) | async-done | bytes 8388640 | tf_op jit(solution)/shard_map/all_to_all | solution.py:70
  170.4 10.0 %convolution_convert_fusion.1 = bf16[1024,512]{1,0:T(8,128)(2,1)} fusion(bf16[1024,4096]{1,0:T(8,128)(2,1)} %bitcast.9, bf16[4096,512]{1,0:T(8,128)(2,1)} %param.15), kind=kOutput, calls=%fused_computation.33 | convolution fusion | flops 4295491584 | bytes 13631488 | tf_op jit(solution)/shard_map/dot_general | solution.py:68
  180.4 9.2 %all-to-all-start.1 = ((bf16[8,128,512]{2,1,0:T(8,128)(2,1)}), bf16[8,128,512]{2,1,0:T(8,128)(2,1)S(1)}, u32[]{:S(2)}, u32[]{:S(2)}) async-start(bf16[8,128,512]{2,1,0:T(8,128)(2,1)} %bitcast.93), calls=%async_computation.1 | async-start | bytes 2097152 | tf_op jit(solution)/shard_map/all_to_all | solution.py:75
  190.2 13.5 %all-to-all-done.1 = bf16[8,128,512]{2,1,0:T(8,128)(2,1)S(1)} async-done(((bf16[8,128,512]{2,1,0:T(8,128)(2,1)}), bf16[8,128,512]{2,1,0:T(8,128)(2,1)S(1)}, u32[]{:S(2)}, u32[]{:S(2)}) %all-to-all-start.1) | async-done | bytes 1048608 | tf_op jit(solution)/shard_map/all_to_all | solution.py:75
  203.7 1.6 convert_bitcast_fusion
  206.4 7.7 gather_fusion
  214.2 18.4 %scatter_custom_fusion = bf16[1152,4096]{1,0:T(8,128)(2,1)} fusion(s32[1024]{0:T(1024)S(1)} %bitcast.97, bf16[1024,4096]{1,0:T(8,128)(2,1)} %gather_fusion, bf16[]{:T(256)} %constant.43.clone.1), kind=kCustom, calls=%fused_computation.18 | custom fusion | bytes 9437696 | tf_op jit(solution)/shard_map/scatter | solution.py:96
  232.5 15.1 %reshape.170 = bf16[128,9,4096]{2,1,0:T(8,128)(2,1)} reshape(bf16[1152,4096]{1,0:T(8,128)(2,1)} %scatter_custom_fusion) | data formatting | bytes 18874368 | tf_op jit(solution)/shard_map/reshape | solution.py:98
  247.7 197.3 %all_to_all.28 = bf16[128,9,4096]{2,1,0:T(8,128)(2,1)} all-to-all(bf16[128,9,4096]{2,1,0:T(8,128)(2,1)} %reshape.170), channel_id=1, replica_groups=mesh['dp'=16,'ctx'=8] {'dp','ctx'}, dimensions={0} | all-to-all | bytes 18874368 | tf_op jit(solution)/shard_map/all_to_all | solution.py:100
  445.0 15.8 %reshape.171 = bf16[1152,4096]{1,0:T(8,128)(2,1)} reshape(bf16[128,9,4096]{2,1,0:T(8,128)(2,1)} %all_to_all.28) | data formatting | bytes 18874368 | tf_op jit(solution)/shard_map/reshape | solution.py:13
  460.8 12.0 %fusion.10 = f32[1152,768]{1,0:T(8,128)S(1)} fusion(bf16[1152,4096]{1,0:T(8,128)(2,1)} %reshape.171, bf16[1,4096,768]{2,1,0:T(8,128)(2,1)} %param.19), kind=kOutput, calls=%fused_computation.16 | convolution fusion | flops 7247757312 | bytes 19267584 | tf_op jit(solution)/shard_map/dot_general | solution.py:14
  472.8 10.3 %fusion.17 = bf16[1152,768]{1,0:T(8,128)(2,1)S(1)} fusion(bf16[1152,4096]{1,0:T(8,128)(2,1)S(1)} %copy-done, bf16[1,4096,768]{2,1,0:T(8,128)(2,1)} %param.20, f32[1152,768]{1,0:T(8,128)S(1)} %fusion.10), kind=kOutput, calls=%fused_computation.21 | convolution fusion | flops 7253065728 | bytes 21037056 | tf_op jit(solution)/shard_map/dot_general | solution.py:15
  483.1 9.6 %convolution_convert_fusion = bf16[1152,4096]{1,0:T(8,128)(2,1)} fusion(bf16[1152,768]{1,0:T(8,128)(2,1)S(1)} %fusion.17, bf16[1,768,4096]{2,1,0:T(8,128)(2,1)S(1)} %bitcast.102), kind=kOutput, calls=%fused_computation.7 | convolution fusion | flops 7252475904 | bytes 17498112 | tf_op jit(solution)/shard_map/dot_general | solution.py:17
  492.7 15.1 %reshape.172 = bf16[128,9,4096]{2,1,0:T(8,128)(2,1)} reshape(bf16[1152,4096]{1,0:T(8,128)(2,1)} %convolution_convert_fusion) | data formatting | bytes 18874368 | tf_op jit(solution)/shard_map/reshape | solution.py:18
  507.8 9.5 %all-to-all-start.3 = ((bf16[128,9,4096]{2,1,0:T(8,128)(2,1)}), bf16[128,9,4096]{2,1,0:T(8,128)(2,1)}, u32[]{:S(2)}, u32[]{:S(2)}) async-start(bf16[128,9,4096]{2,1,0:T(8,128)(2,1)} %reshape.172), calls=%async_computation.3 | async-start | bytes 33554432 | tf_op jit(solution)/shard_map/all_to_all | solution.py:105
  517.5 4.2 copy.25
  521.7 2.7 reshape.174
  524.4 222.0 %all-to-all-done.3 = bf16[128,9,4096]{2,1,0:T(8,128)(2,1)} async-done(((bf16[128,9,4096]{2,1,0:T(8,128)(2,1)}), bf16[128,9,4096]{2,1,0:T(8,128)(2,1)}, u32[]{:S(2)}, u32[]{:S(2)}) %all-to-all-start.3) | async-done | bytes 9437216 | tf_op jit(solution)/shard_map/all_to_all | solution.py:105
  746.5 15.8 %reshape.173 = bf16[1152,4096]{1,0:T(8,128)(2,1)} reshape(bf16[128,9,4096]{2,1,0:T(8,128)(2,1)} %all-to-all-done.3) | data formatting | bytes 18874368 | tf_op jit(solution)/shard_map/reshape | solution.py:106
  762.3 20.0 %gather_fusion.1 = bf16[1024,4096]{1,0:T(8,128)(2,1)} fusion(bf16[1152,4096]{1,0:T(8,128)(2,1)} %reshape.173, s32[1024]{0:T(1024)S(1)} %broadcast_clamp_fusion), kind=kCustom, calls=%fused_computation.1 | custom fusion | bytes 16781312 | tf_op jit(solution)/shard_map/gather | solution.py:107
  782.3 13.2 %fusion = f32[128,4096]{1,0:T(8,128)} fusion(bf16[1024,4096]{1,0:T(8,128)(2,1)} %gather_fusion.1, f32[128,8]{1,0:T(8,128)S(1)} %copy.26), kind=kLoop, calls=%fused_computation.4 | loop fusion | flops 12058624 | bytes 10489856 | tf_op jit(solution)/shard_map/reduce_sum | solution.py:108
  795.5 3.5 fusion.21
  (44 shorter events, 2.8 us)
Async XLA Ops:
  74.1 6.0 copy-start.3
  74.1 96.3 %all-to-all-start = ((bf16[8,128,4096]{2,1,0:T(8,128)(2,1)}), bf16[8,128,4096]{2,1,0:T(8,128)(2,1)}, u32[]{:S(2)}, u32[]{:S(2)}) async-start(bf16[8,128,4096]{2,1,0:T(8,128)(2,1)} %stack.2), calls=%async_computation | async-start | bytes 16777216 | tf_op jit(solution)/shard_map/all_to_all | solution.py:70
  180.4 25.1 %copy-start.1 = (bf16[1,128,4096]{2,1,0:T(8,128)(2,1)S(1)}, bf16[1,128,4096]{2,1,0:T(8,128)(2,1)}, u32[]{:S(2)}) copy-start(bf16[1,128,4096]{2,1,0:T(8,128)(2,1)} %param.11) | copy-start | bytes 3145732
  180.4 25.6 %copy-start.2 = (f32[4096]{0:T(1024)S(1)}, f32[4096]{0:T(1024)}, u32[]{:S(2)}) copy-start(f32[4096]{0:T(1024)} %param.16) | copy-start | bytes 49156
  180.4 23.3 %all-to-all-start.1 = ((bf16[8,128,512]{2,1,0:T(8,128)(2,1)}), bf16[8,128,512]{2,1,0:T(8,128)(2,1)S(1)}, u32[]{:S(2)}, u32[]{:S(2)}) async-start(bf16[8,128,512]{2,1,0:T(8,128)(2,1)} %bitcast.93), calls=%async_computation.1 | async-start | bytes 2097152 | tf_op jit(solution)/shard_map/all_to_all | solution.py:75
  460.8 12.0 %copy-start = (bf16[1152,4096]{1,0:T(8,128)(2,1)S(1)}, bf16[1152,4096]{1,0:T(8,128)(2,1)}, u32[]{:S(2)}) copy-start(bf16[1152,4096]{1,0:T(8,128)(2,1)} %reshape.171) | copy-start | bytes 28311556
  460.8 22.3 %slice-start = ((s8[6291456]{0:T(1024)(128)(4,1)}), s8[4194304]{0:T(1024)(128)(4,1)S(1)}, s32[]{:S(2)}) async-start(s8[6291456]{0:T(1024)(128)(4,1)} %bitcast.101), calls=%async_computation.4 | async-start | bytes 8388608
  472.8 10.3 %slice-start.1 = ((s8[6291456]{0:T(1024)(128)(4,1)}), s8[2097152]{0:T(1024)(128)(4,1)S(1)}, s32[]{:S(2)}) async-start(s8[6291456]{0:T(1024)(128)(4,1)} %bitcast.101), calls=%async_computation.5 | async-start | bytes 4194304
  507.8 9.6 %copy-start.4 = (f32[1,128,8]{1,2,0:T(8,128)S(1)}, f32[1,128,8]{1,2,0:T(8,128)}, u32[]{:S(2)}) copy-start(f32[1,128,8]{1,2,0:T(8,128)} %param.18) | copy-start | bytes 12292
  507.8 238.7 %all-to-all-start.3 = ((bf16[128,9,4096]{2,1,0:T(8,128)(2,1)}), bf16[128,9,4096]{2,1,0:T(8,128)(2,1)}, u32[]{:S(2)}, u32[]{:S(2)}) async-start(bf16[128,9,4096]{2,1,0:T(8,128)(2,1)} %reshape.172), calls=%async_computation.3 | async-start | bytes 33554432 | tf_op jit(solution)/shard_map/all_to_all | solution.py:105
